TPU v7x, 512 devices: a whole 4x8x8 slice. The times are simulated.
512 devices in a mesh: row: 128 (over z, y, core), ex: 4 (over x).
Axes of the slice: x: 4, y: 8, z: 8, core: 2. Of those that a mesh axis runs over, the one named last changes fastest.
Arguments:
- grads: bfloat16 [1, 4, 2048, 2048], P(None, 'ex', 'row'), may hold values from -6 to 6
- right_inv: bfloat16 [2048, 2048], P('row', 'ex'), may hold values from -0.125 to 0.125
- left_inv: bfloat16 [2048, 2048], P(('row', 'ex')), may hold values from -0.125 to 0.125
- row_signs: int32 [1, 4, 2048], replicated, may hold values from 0 to 1
- col_signs: int32 [1, 4, 2048], replicated, may hold values from 0 to 1
- listed: int32 [1, 128, 4, 32], P(None, 'row', 'ex'), may hold values from 0 to 32767, as said below
- owners: int32 [1, 128, 4, 32, 1], P(None, 'row'), may hold values from 0 to 127; in each aligned block of 128 rows (0 to 127, 128 to 255, ..., all dimensions but the last counted through in order) at most 2 rows name the same one
Outputs:
- sketch: float32 [1, 128, 128, 2, 256], P(None, 'row')
Inputs may be any that keep to these rules, and one draw needn't show every extreme that they name: `listed`: for each batch b, group g and example x, the 32 entries name distinct blocks in ascending order, all from g * 256 to (g + 1) * 256 - 1. `owners`: within one batch and group, no owner is named by more than 2 of the 128 entries, a bound that some block reaches.
All inputs are finite; a program needn't handle non-finite values.
Results may differ from a plain program's by a relative error of at most 0.0029.
Values may be sent and summed in bfloat16 or wider, within the bound.
No kernel may reach another device: no remote copies, remote signals or barrier semaphores. Data moves between devices by JAX's collectives and lax.ppermute only.
A program may use at most 64 MiB of HBM per device.

v0:
```python
import math

import jax
import jax.numpy as jnp
from jax import lax
from jax.sharding import PartitionSpec as P

FA = 32
FB = 64
BLOCK = 128


highest = lax.Precision.HIGHEST


def dft_tables(length):
    counter = jnp.arange(length, dtype=jnp.int32)
    phase_index = counter[:, None] * counter[None, :] % length
    angles = phase_index.astype(jnp.float32) * (2.0 * math.pi / length)
    return (jnp.cos(angles), -jnp.sin(angles))


def twiddle_table(first_len, second_len, total):
    phase_index = (
        jnp.arange(first_len, dtype=jnp.int32)[:, None]
        * jnp.arange(second_len, dtype=jnp.int32)[None, :]
    )
    angles = phase_index.astype(jnp.float32) * (2.0 * math.pi / total)
    return (jnp.cos(angles), -jnp.sin(angles))


def complex_mul(real_a, imag_a, real_b, imag_b):
    return (real_a * real_b - imag_a * imag_b, real_a * imag_b + imag_a * real_b)


def column_transform(flipped, tables):
    first_cos, first_sin, mid_cos, mid_sin, last_cos, last_sin = tables
    lanes = flipped.shape[0]
    spatial = flipped.reshape(lanes, FA, FB)
    real_one = jnp.einsum("pk,jpq->jkq", first_cos, spatial, precision=highest)
    imag_one = jnp.einsum("pk,jpq->jkq", first_sin, spatial, precision=highest)
    real_two, imag_two = complex_mul(real_one, imag_one, mid_cos[None], mid_sin[None])
    real_out = jnp.einsum("qm,jkq->jmk", last_cos, real_two, precision=highest) - jnp.einsum(
        "qm,jkq->jmk", last_sin, imag_two, precision=highest
    )
    imag_out = jnp.einsum("qm,jkq->jmk", last_sin, real_two, precision=highest) + jnp.einsum(
        "qm,jkq->jmk", last_cos, imag_two, precision=highest
    )
    return (real_out.reshape(lanes, FA * FB), imag_out.reshape(lanes, FA * FB))


def row_transform(real_in, imag_in, tables):
    first_cos, first_sin, mid_cos, mid_sin, last_cos, last_sin = tables
    lanes = real_in.shape[1]
    real_grid = real_in.reshape(FA, FB, lanes)
    imag_grid = imag_in.reshape(FA, FB, lanes)
    real_one = jnp.einsum("pk,pql->kql", first_cos, real_grid, precision=highest) - jnp.einsum(
        "pk,pql->kql", first_sin, imag_grid, precision=highest
    )
    imag_one = jnp.einsum("pk,pql->kql", first_sin, real_grid, precision=highest) + jnp.einsum(
        "pk,pql->kql", first_cos, imag_grid, precision=highest
    )
    real_two, imag_two = complex_mul(real_one, imag_one, mid_cos[:, :, None], mid_sin[:, :, None])
    real_out = jnp.einsum("qm,kql->lmk", last_cos, real_two, precision=highest) - jnp.einsum(
        "qm,kql->lmk", last_sin, imag_two, precision=highest
    )
    imag_out = jnp.einsum("qm,kql->lmk", last_sin, real_two, precision=highest) + jnp.einsum(
        "qm,kql->lmk", last_cos, imag_two, precision=highest
    )
    return (real_out.reshape(lanes, FA * FB), imag_out.reshape(lanes, FA * FB))


def shards(grads, right_inv, left_inv, row_signs, col_signs, listed, owners):
    row_count = lax.axis_size("row")
    ex_count = lax.axis_size("ex")
    row_id = lax.axis_index("row")
    ex_id = lax.axis_index("ex")
    local_rows = grads.shape[2]
    width = grads.shape[3]
    ex_cols = right_inv.shape[1]
    list_len = listed.shape[3]
    block_count = local_rows * (width // BLOCK)
    capacity = max(2, 2 * ex_count * list_len // row_count)
    right_cols = lax.all_gather(right_inv, "row", axis=0, tiled=True)
    left_full = lax.all_gather(left_inv, ("row", "ex"), axis=0, tiled=True)
    pair_start = row_id * local_rows
    my_example = pair_start // ex_cols
    col_start = ex_id * ex_cols + pair_start % ex_cols
    first_cos, first_sin = dft_tables(FA)
    mid_cos, mid_sin = twiddle_table(FA, FB, width)
    last_cos, last_sin = dft_tables(FB)
    tables = (first_cos, first_sin, mid_cos, mid_sin, last_cos, last_sin)
    columns = col_start + jnp.arange(local_rows, dtype=jnp.int32)
    cross_phase = columns[:, None] * jnp.arange(width, dtype=jnp.int32)[None, :]
    cross_angle = cross_phase.astype(jnp.float32) * (2.0 * math.pi / (width * width))
    cross_cos = jnp.cos(cross_angle)
    cross_sin = -jnp.sin(cross_angle)
    entry_order = jnp.arange(ex_count * list_len, dtype=jnp.int32)
    before = entry_order[:, None] < entry_order[None, :]
    own_rows = grads[0]
    rows_all = lax.all_gather(own_rows, "ex", axis=0, tiled=True)
    projected = jnp.einsum(
        "xrk,kc->xcr", rows_all, right_cols, preferred_element_type=jnp.float32
    ).astype(jnp.bfloat16)
    projected = projected.reshape(ex_count * ex_cols, local_rows)
    pair_cols = lax.all_to_all(projected, "row", split_axis=0, concat_axis=1, tiled=True)
    whitened = lax.dot_general(
        pair_cols, left_full, (((1,), (1,)), ((), ())), preferred_element_type=jnp.float32
    )
    row_bits = lax.dynamic_index_in_dim(row_signs[0], my_example, 0, keepdims=False)
    col_bits = lax.dynamic_slice(col_signs[0], (my_example, col_start), (1, local_rows))[0]
    row_flip = (1 - 2 * row_bits).astype(jnp.float32)
    col_flip = (1 - 2 * col_bits).astype(jnp.float32)
    flipped = whitened * row_flip[None, :] * col_flip[:, None]
    real_one, imag_one = column_transform(flipped, tables)
    real_two, imag_two = complex_mul(real_one, imag_one, cross_cos, cross_sin)
    stacked = jnp.stack([real_two, imag_two])
    arrived_rows = lax.all_to_all(
        lax.all_to_all(stacked, "row", split_axis=2, concat_axis=1, tiled=True),
        "ex",
        split_axis=1,
        concat_axis=1,
        tiled=True,
    )
    real_four, imag_four = row_transform(arrived_rows[0], arrived_rows[1], tables)
    real_four = real_four / width
    imag_four = imag_four / width
    packed = jnp.concatenate(
        [real_four.reshape(block_count, BLOCK), imag_four.reshape(block_count, BLOCK)], axis=1
    )
    local_ids = listed[0, 0, 0] - row_id * block_count
    picked = jnp.take(packed, local_ids, axis=0)
    entries = lax.all_gather(picked, "ex", axis=0, tiled=True)
    owner_ids = owners[0, 0, :, :, 0].reshape(-1)
    same = owner_ids[:, None] == owner_ids[None, :]
    slot_index = jnp.sum(same & before, axis=0)
    position = owner_ids * capacity + slot_index
    outgoing = jnp.zeros((row_count * capacity, 2 * BLOCK), jnp.float32).at[position].set(entries)
    arrived = lax.all_to_all(outgoing, "row", split_axis=0, concat_axis=0, tiled=True)
    stores = [arrived.reshape(1, row_count, capacity, 2 * BLOCK)]
    return jnp.stack(stores)


def solution(mesh):
    in_specs = (
        P(None, "ex", "row", None),
        P("row", "ex"),
        P(("row", "ex"), None),
        P(),
        P(),
        P(None, "row", "ex", None),
        P(None, "row", None, None, None),
    )
    out_specs = P(None, "row", None, None, None)
    return jax.shard_map(shards, mesh=mesh, in_specs=in_specs, out_specs=out_specs, check_vma=False)
```

profile of v0, /device:TPU:1, one launch (start us, length us, event | category | flops | bytes accessed | tf_op | source)
XLA Modules:
  0.0 361.3 jit_solution(6742715925657476330)
XLA Ops:
  6.5 0.7 all-gather.5.cloned.1.call-update
  7.3 0.7 all-gather.7.cloned.1.call-update
  8.0 10.7 %all-gather = bf16[4,1,16,2048]{3,2,1,0:T(8,128)(2,1)S(1)} all-gather(bf16[1,1,16,2048]{3,2,1,0:T(8,128)(2,1)} %param.7), channel_id=2, replica_groups=mesh['row'=128,'ex'=4] {'ex'}, dimensions={0}, use_global_device_ids=true | all-gather | bytes 327680 | tf_op jit(solution)/shard_map/all_gather | solution.py:101
  18.8 0.7 fusion.70
  19.5 0.8 subtract_convert_fusion
  20.2 79.2 %all-gather.5.cloned.1.call-done = bf16[2048,512]{1,0:T(8,128)(2,1)} async-done(((bf16[16,512]{1,0:T(8,128)(2,1)}), bf16[2048,512]{1,0:T(8,128)(2,1)}) %all-gather.5.cloned.1.call-update) | async-done | bytes 2097168 | tf_op jit(solution)/shard_map/all_gather | solution.py:84
  99.4 2.1 fusion.12
  101.6 0.4 all_to_all.36
  101.9 0.3 copy.52
  102.3 1.0 reshape.326
  103.3 9.4 %all-to-all-start = ((bf16[128,2,128]{2,1,0:T(2,128)(2,1)}), bf16[128,2,128]{2,1,0:T(2,128)(2,1)S(1)}, u32[]{:S(2)}, u32[]{:S(2)}) async-start(bf16[128,2,128]{2,1,0:T(2,128)(2,1)} %reshape.326), calls=%async_computation | async-start | bytes 131072 | tf_op jit(solution)/shard_map/all_to_all | solution.py:106
  112.7 0.8 convert_bitcast_fusion
  113.6 10.6 %all-to-all-done = bf16[128,2,128]{2,1,0:T(2,128)(2,1)S(1)} async-done(((bf16[128,2,128]{2,1,0:T(2,128)(2,1)}), bf16[128,2,128]{2,1,0:T(2,128)(2,1)S(1)}, u32[]{:S(2)}, u32[]{:S(2)}) %all-to-all-start) | async-done | bytes 65568 | tf_op jit(solution)/shard_map/all_to_all | solution.py:106
  124.1 0.4 reshape.327
  124.5 104.7 %all-gather.7.cloned.1.call-done = bf16[512,4,2048]{2,1,0:T(4,128)(2,1)} async-done(((bf16[1,4,2048]{2,1,0:T(4,128)(2,1)}), bf16[512,4,2048]{2,1,0:T(4,128)(2,1)}) %all-gather.7.cloned.1.call-update) | async-done | bytes 8388624 | tf_op jit(solution)/shard_map/all_gather | solution.py:85
  229.2 12.5 %reshape.304 = bf16[2048,2048]{1,0:T(8,128)(2,1)} reshape(bf16[512,4,2048]{2,1,0:T(4,128)(2,1)} %all-gather.7.cloned.1.call-done) | data formatting | bytes 16777216
  241.7 5.6 %fusion = f32[16,2048]{1,0:T(8,128)S(1)} fusion(bf16[16,2048]{0,1:T(8,128)(2,1)S(1)} %bitcast.111, bf16[2048,2048]{1,0:T(8,128)(2,1)} %reshape.304, f32[16]{0:T(128)S(1)} %convert_bitcast_fusion, f32[2048]{0:T(1024)S(1)} %bitcast.113), kind=kOutput, calls=%fused_computation.3 | convolution fusion | flops 134283264 | bytes 8593472 | tf_op jit(solution)/shard_map/dot_general | solution.py:107
  247.5 0.5 convolution_bitcast_fusion
  247.9 0.4 convolution_bitcast_fusion.1
  248.4 0.5 fusion.20
  248.9 0.5 fusion.19
  249.4 0.5 fusion.8
  249.9 0.2 copy.33
  250.1 0.2 reshape.284
  250.4 0.5 fusion.7
  250.9 0.2 copy.34
  251.1 0.2 reshape.285
  251.3 0.6 multiply_subtract_fusion.2
  252.0 1.0 copy.35
  253.0 3.6 reshape.328
  256.6 10.0 %all-to-all-start.1 = ((f32[128,1,512]{2,1,0:T(1,128)}), f32[128,1,512]{2,1,0:T(1,128)S(1)}, u32[]{:S(2)}, u32[]{:S(2)}) async-start(f32[128,1,512]{2,1,0:T(1,128)} %reshape.328), calls=%async_computation.1 | async-start | bytes 524288 | tf_op jit(solution)/shard_map/all_to_all | solution.py:119
  266.6 0.5 broadcast.267
  267.1 0.7 fusion.127
  268.1 13.7 %all-to-all-done.1 = f32[128,1,512]{2,1,0:T(1,128)S(1)} async-done(((f32[128,1,512]{2,1,0:T(1,128)}), f32[128,1,512]{2,1,0:T(1,128)S(1)}, u32[]{:S(2)}, u32[]{:S(2)}) %all-to-all-start.1) | async-done | bytes 262176 | tf_op jit(solution)/shard_map/all_to_all | solution.py:119
  281.8 0.5 broadcast.268
  282.3 1.2 reduce.9
  283.6 2.8 reshape.329
  286.4 2.6 copy.51
  288.9 3.2 copy.46
  292.2 3.6 reshape.330
  295.8 3.7 %all-to-all-start.2 = ((f32[4,1,16384]{2,1,0:T(1,128)}), f32[4,1,16384]{2,1,0:T(1,128)S(1)}, u32[]{:S(2)}, u32[]{:S(2)}) async-start(f32[4,1,16384]{2,1,0:T(1,128)} %reshape.330), calls=%async_computation.2 | async-start | bytes 524288 | tf_op jit(solution)/shard_map/all_to_all | solution.py:118
  299.5 5.8 %all-to-all-done.2 = f32[4,1,16384]{2,1,0:T(1,128)S(1)} async-done(((f32[4,1,16384]{2,1,0:T(1,128)}), f32[4,1,16384]{2,1,0:T(1,128)S(1)}, u32[]{:S(2)}, u32[]{:S(2)}) %all-to-all-start.2) | async-done | bytes 262176 | tf_op jit(solution)/shard_map/all_to_all | solution.py:118
  305.3 1.3 reduce.10
  306.6 2.8 reshape.331
  309.4 2.4 fusion.128
  311.9 1.6 copy.47
  313.5 0.4 fusion.46
  313.9 0.4 fusion.41
  314.3 0.4 copy.48
  314.7 0.4 convolution_subtract_fusion.1
  315.2 0.4 convolution_add_fusion.1
  315.6 0.5 fusion.22
  316.1 0.5 fusion.21
  316.6 0.5 fusion.6
  317.1 0.2 copy.41
  317.3 0.2 div.27
  317.5 0.5 fusion.4
  318.0 0.2 copy.42
  318.2 0.2 div.30
  318.4 0.6 gather_fusion
  319.1 9.5 %all_gather.15 = f32[128,256]{1,0:T(8,128)S(1)} all-gather(f32[32,256]{1,0:T(8,128)S(1)} %broadcast_select_fusion), channel_id=1, replica_groups=mesh['row'=128,'ex'=4] {'ex'}, dimensions={0}, use_global_device_ids=true | all-gather | bytes 163840 | tf_op jit(solution)/shard_map/all_gather | solution.py:133
  328.6 1.1 scatter_custom_fusion
  329.8 24.0 %all_to_all.51 = f32[128,2,256]{2,1,0:T(2,128)S(1)} all-to-all(f32[128,2,256]{2,1,0:T(2,128)S(1)} %all_to_all.45), channel_id=1, replica_groups=mesh['row'=128,'ex'=4] {'row'}, dimensions={0} | all-to-all | bytes 524288 | tf_op jit(solution)/shard_map/all_to_all | solution.py:139
  353.8 0.7 copy.54
  (20 shorter events, 0.9 us)
Async XLA Ops:
  6.5 92.9 %all-gather.5.cloned.1.call-start = ((), (), s32[]{:S(2)}) async-start(), calls=%async_computation.4 | async-start | bytes 2113536 | tf_op jit(solution)/shard_map/all_gather | solution.py:84
  7.3 222.0 %all-gather.7.cloned.1.call-start = ((), (), s32[]{:S(2)}) async-start(), calls=%async_computation.5 | async-start | bytes 8404992 | tf_op jit(solution)/shard_map/all_gather | solution.py:85
  103.3 20.9 %all-to-all-start = ((bf16[128,2,128]{2,1,0:T(2,128)(2,1)}), bf16[128,2,128]{2,1,0:T(2,128)(2,1)S(1)}, u32[]{:S(2)}, u32[]{:S(2)}) async-start(bf16[128,2,128]{2,1,0:T(2,128)(2,1)} %reshape.326), calls=%async_computation | async-start | bytes 131072 | tf_op jit(solution)/shard_map/all_to_all | solution.py:106
  251.9 15.2 %copy-start = (s32[1,1,4,32,1]{3,4,2,1,0:T(1,128)S(1)}, s32[1,1,4,32,1]{3,4,2,1,0:T(1,128)}, u32[]{:S(2)}) copy-start(s32[1,1,4,32,1]{3,4,2,1,0:T(1,128)} %param.13) | copy-start | bytes 1540
  256.6 25.2 %all-to-all-start.1 = ((f32[128,1,512]{2,1,0:T(1,128)}), f32[128,1,512]{2,1,0:T(1,128)S(1)}, u32[]{:S(2)}, u32[]{:S(2)}) async-start(f32[128,1,512]{2,1,0:T(1,128)} %reshape.328), calls=%async_computation.1 | async-start | bytes 524288 | tf_op jit(solution)/shard_map/all_to_all | solution.py:119
  292.2 7.3 %copy-start.1 = (s32[1,1,1,32]{3,2,1,0:T(1,128)S(1)}, s32[1,1,1,32]{3,2,1,0:T(1,128)}, u32[]{:S(2)}) copy-start(s32[1,1,1,32]{3,2,1,0:T(1,128)} %param.12) | copy-start | bytes 388
  295.8 9.5 %all-to-all-start.2 = ((f32[4,1,16384]{2,1,0:T(1,128)}), f32[4,1,16384]{2,1,0:T(1,128)S(1)}, u32[]{:S(2)}, u32[]{:S(2)}) async-start(f32[4,1,16384]{2,1,0:T(1,128)} %reshape.330), calls=%async_computation.2 | async-start | bytes 524288 | tf_op jit(solution)/shard_map/all_to_all | solution.py:118
Sparse Core Ops, SparseCore 0:
  10.5 88.9 all-gather.4
  103.9 125.2 all-gather.6
where the time goes:
time: 362 us; the launch traced here: 361 us
  waiting for transfers between devices  215 us (59%)
  blocking collectives  44.2 us (12%)
  local copies, waits for them, and re-layouts  44.1 us (12%)
  starting transfers between devices  23.1 us (6%)
  matrix products  14.3 us (4%)
  between operations  13.8 us (4%)
  other arithmetic  6.33 us (2%)
    all_gather x1, waiting for transfers between devices, shards(): left_full = lax.all_gather(left_inv, ('row', 'ex'), axis=0, tiled=True)  105 us
    all_gather x1, waiting for transfers between devices, shards(): right_cols = lax.all_gather(right_inv, 'row', axis=0, tiled=True)  79.2 us
    unnamed x13, local copies, waits for them, and re-layouts  27.9 us
    all_to_all x1, blocking collectives, shards(): lax.all_to_all(outgoing, 'row', split_axis=0, concat_axis=0, tiled=True)  24 us
    all_to_all x1, waiting for transfers between devices, shards(): lax.all_to_all(stacked, 'row', split_axis=2, concat_axis=1, tiled=True)  13.7 us
    all_gather x1, blocking collectives, shards(): rows_all = lax.all_gather(own_rows, 'ex', axis=0, tiled=True)  10.7 us
    all_to_all x1, waiting for transfers between devices, shards(): lax.all_to_all(projected, 'row', split_axis=0, concat_axis=1, tiled=True)  10.6 us
    all_to_all x1, starting transfers between devices, shards(): lax.all_to_all(stacked, 'row', split_axis=2, concat_axis=1, tiled=True)  9.99 us
  transfers between devices with their start and end apart: 5, of which 5 were waited for; matrix products, arithmetic and copies ran while one was open for 2% of the time, Pallas kernels for 0%

commit v1 on v0

v1 whole, which is shorter than its diff:
```python
import math

import jax
import jax.numpy as jnp
import numpy as np
from jax import lax
from jax.experimental import pallas as pl
from jax.experimental.pallas import tpu as pltpu
from jax.sharding import Mesh
from jax.sharding import PartitionSpec as P

DM = 2048
BLOCK = 128
NZ, NY, NC, NE = 8, 8, 2, 4
NYC = NY * NC
ROWS = NZ * NYC
GROUP_ROWS = DM // ROWS
TILE_ROWS = DM // NZ
RADIX = 8
INNER = DM // RADIX
ROOT_HALF = math.sqrt(0.5)

f32 = jnp.float32
bf16 = jnp.bfloat16
ROW_AXES = ("z", "y", "c")


def split_table(table):
    high = table.astype(bf16)
    low = (table - high.astype(np.float64)).astype(bf16)
    return high, low


def dft_angles(rows, cols, length):
    return 2.0 * math.pi * ((np.arange(rows)[:, None] * np.arange(cols)[None, :]) % length) / length


def column_tables():
    angles = dft_angles(INNER, INNER, INNER)
    high, low = split_table(np.concatenate([np.cos(angles), -np.sin(angles)], axis=0))
    angles = dft_angles(INNER, RADIX, DM)
    twiddles = np.concatenate([np.cos(angles), -np.sin(angles)], axis=1).astype(np.float32)
    return high, low, twiddles


def row_tables():
    angles = dft_angles(BLOCK, BLOCK, BLOCK)
    real, imag = np.cos(angles), -np.sin(angles)
    full = np.concatenate(
        [np.concatenate([real, imag], axis=1), np.concatenate([-imag, real], axis=1)], axis=0
    )
    high, low = split_table(full)
    angles = dft_angles(NYC, BLOCK, DM)
    twiddles = np.stack([np.cos(angles), -np.sin(angles)]).astype(np.float32)
    return high, low, twiddles.reshape(2, NYC, 1, BLOCK)


def add(a, b):
    return (a[0] + b[0], a[1] + b[1])


def sub(a, b):
    return (a[0] - b[0], a[1] - b[1])


def mul(a, b):
    return (a[0] * b[0] - a[1] * b[1], a[0] * b[1] + a[1] * b[0])


def minus_i(a):
    return (a[1], -a[0])


def fft4(a, b, c, d):
    even, odd = add(a, c), sub(a, c)
    even2, odd2 = add(b, d), minus_i(sub(b, d))
    return [add(even, even2), add(odd, odd2), sub(even, even2), sub(odd, odd2)]


def fft8(terms):
    even = fft4(terms[0], terms[2], terms[4], terms[6])
    odd = fft4(terms[1], terms[3], terms[5], terms[7])
    one = ((odd[1][0] + odd[1][1]) * ROOT_HALF, (odd[1][1] - odd[1][0]) * ROOT_HALF)
    three = ((odd[3][1] - odd[3][0]) * ROOT_HALF, (odd[3][0] + odd[3][1]) * -ROOT_HALF)
    turned = [odd[0], one, minus_i(odd[2]), three]
    return [add(e, o) for e, o in zip(even, turned)] + [sub(e, o) for e, o in zip(even, turned)]


def fft16(terms):
    inner = [fft4(*[terms[4 * a + b] for a in range(4)]) for b in range(4)]
    out = [None] * 16
    for first in range(4):
        column = []
        for b in range(4):
            turn = -2.0 * math.pi * b * first / 16
            value = inner[b][first]
            if b * first:
                cos, sin = math.cos(turn), math.sin(turn)
                value = (value[0] * cos - value[1] * sin, value[0] * sin + value[1] * cos)
            column.append(value)
        for second, value in enumerate(fft4(*column)):
            out[first + 4 * second] = value
    return out


def dot(a, b):
    return jnp.dot(a, b, preferred_element_type=f32)


def whiten_kernel(gg, rl, lx, row_flip, col_flip, high, low, twiddles, out, white, stage):
    right = rl[:, 0:GROUP_ROWS, :].reshape(DM, BLOCK)
    projected = dot(gg[...].reshape(TILE_ROWS, DM), right) * col_flip[...]
    projected = projected.astype(bf16).reshape(NC, NY, GROUP_ROWS, BLOCK)
    tile = jnp.concatenate([projected[c, y] for y in range(NY) for c in range(NC)], axis=0)
    left = jnp.concatenate([lx[0].reshape(DM, BLOCK), lx[1].reshape(DM, BLOCK)], axis=1)
    white[...] = dot(left, tile) * row_flip[...]
    for p in range(RADIX):
        part = white[pl.ds(p, INNER, stride=RADIX), :]
        part_high = part.astype(bf16)
        part_low = (part - part_high.astype(f32)).astype(bf16)
        stage[p] = dot(high[...], part_high) + dot(low[...], part_high) + dot(high[...], part_low)

    def combine(step, carry):
        rows = pl.ds(pl.multiple_of(step * GROUP_ROWS, GROUP_ROWS), GROUP_ROWS)
        rows_imag = pl.ds(pl.multiple_of(INNER + step * GROUP_ROWS, GROUP_ROWS), GROUP_ROWS)
        factors = twiddles[rows, :]
        terms = [(stage[0, rows, :], stage[0, rows_imag, :])]
        for p in range(1, RADIX):
            factor = (factors[:, p : p + 1], factors[:, RADIX + p : RADIX + p + 1])
            terms.append(mul((stage[p, rows, :], stage[p, rows_imag, :]), factor))
        for k, value in enumerate(fft8(terms)):
            out[NYC * k + step, 0:GROUP_ROWS, :] = value[0].astype(bf16)
            out[NYC * k + step, GROUP_ROWS : 2 * GROUP_ROWS, :] = value[1].astype(bf16)
        return carry

    lax.fori_loop(0, INNER // GROUP_ROWS, combine, 0)


def spectrum_kernel(parts, cross, turns, high, low, chosen, block_of, spread, out, mixed):
    terms = []
    for yc in range(NYC):
        total = parts[yc].astype(f32)
        for z in range(1, NZ):
            total = total + parts[z * NYC + yc].astype(f32)
        terms.append(
            mul((total[0:GROUP_ROWS], total[GROUP_ROWS:]), (cross[0, yc], cross[1, yc]))
        )
    for k, value in enumerate(fft16(terms)):
        value = mul(value, (turns[0, k], turns[1, k]))
        mixed[k, :, 0:BLOCK] = value[0]
        mixed[k, :, BLOCK : 2 * BLOCK] = value[1]
    rows = mixed[...].reshape(NYC * GROUP_ROWS, 2 * BLOCK)
    rows_high = rows.astype(bf16)
    rows_low = (rows - rows_high.astype(f32)).astype(bf16)
    result = dot(rows_high, high[...]) + dot(rows_low, high[...]) + dot(rows_high, low[...])
    picked = dot(chosen[...], result.astype(bf16))
    count = picked.shape[0] // NYC
    lane_block = lax.broadcasted_iota(jnp.int32, (NYC * count, BLOCK), 1) // (BLOCK // NYC)
    keep = lane_block == block_of[...]
    sides = []
    for side in range(2):
        own = jnp.where(keep, picked[:, side * BLOCK : (side + 1) * BLOCK], 0.0).astype(bf16)
        own = own.reshape(NYC, count, BLOCK)
        wide = jnp.concatenate([own[k] for k in range(NYC)], axis=1)
        sides.append(dot(wide, spread[...]))
    out[...] = jnp.concatenate(sides, axis=1).astype(bf16)


def shards(grads, right_inv, left_inv, row_signs, col_signs, listed, owners):
    z_id, y_id, c_id, e_id = (lax.axis_index(name) for name in ("z", "y", "c", "e"))
    yc_id = y_id * NC + c_id
    row_id = z_id * NYC + yc_id
    list_len = listed.shape[3]
    capacity = 2

    right_pieces = right_inv.reshape(GROUP_ROWS, NE, BLOCK).transpose(1, 0, 2)
    left_pieces = left_inv.reshape(NE, NYC, BLOCK).transpose(1, 0, 2)
    shared = jnp.concatenate(
        [right_pieces.reshape(NE * GROUP_ROWS, BLOCK), left_pieces.reshape(NYC * NE, BLOCK)], axis=0
    )
    shared = jnp.broadcast_to(shared[None], (NE,) + shared.shape)
    shared = lax.all_to_all(shared, "e", 0, 0, tiled=True)
    right_all = shared[:, : NE * GROUP_ROWS].reshape(NYC, GROUP_ROWS, BLOCK)
    left_all = shared[:, NE * GROUP_ROWS :].reshape(NE, NYC, NE, BLOCK).transpose(1, 0, 2, 3)
    left_all = left_all.reshape(NZ, 1, NC, GROUP_ROWS, BLOCK)
    right_all = right_all.reshape(1, NY, NC, GROUP_ROWS, BLOCK)
    whole = (NZ, NY, NC, GROUP_ROWS, BLOCK)
    factors = jnp.concatenate(
        [jnp.broadcast_to(right_all, whole), jnp.broadcast_to(left_all, whole)], axis=3
    ).reshape(ROWS, 2 * GROUP_ROWS, BLOCK)
    factors = lax.all_to_all(factors, ROW_AXES, 0, 0, tiled=True)

    rows = jnp.broadcast_to(grads.reshape(1, GROUP_ROWS, DM), (NY, GROUP_ROWS, DM))
    rows = lax.all_to_all(rows, "y", 0, 0, tiled=True)
    rows = lax.all_to_all(
        jnp.broadcast_to(rows[None], (NC,) + rows.shape), "c", 0, 0, tiled=True
    )
    left_half = factors[:, GROUP_ROWS:]
    left_cols = lax.all_to_all(
        jnp.broadcast_to(left_half[None], (NC,) + left_half.shape), "c", 0, 0, tiled=True
    )

    row_bits = lax.dynamic_index_in_dim(row_signs[0], e_id, 0, keepdims=False)
    col_bits = lax.dynamic_slice(col_signs[0], (e_id, yc_id * BLOCK), (1, BLOCK))
    row_flip = (1 - 2 * row_bits).astype(f32)[:, None]
    col_flip = (1 - 2 * col_bits).astype(f32)
    high, low, twiddles = column_tables()
    partial_cols = pl.pallas_call(
        whiten_kernel,
        out_shape=jax.ShapeDtypeStruct((ROWS, 2 * GROUP_ROWS, BLOCK), bf16),
        scratch_shapes=[
            pltpu.VMEM((DM, BLOCK), f32),
            pltpu.VMEM((RADIX, 2 * INNER, BLOCK), f32),
        ],
        name="whiten",
    )(rows, factors, left_cols, row_flip, col_flip, high, low, twiddles)
    partial_rows = lax.all_to_all(partial_cols, ROW_AXES, 0, 0, tiled=True)

    spectrum_rows = row_id * GROUP_ROWS + jnp.arange(GROUP_ROWS, dtype=jnp.int32)
    columns = jnp.arange(DM, dtype=jnp.int32).reshape(NYC, 1, BLOCK)
    phase = spectrum_rows[None, :, None] * columns
    angle = phase.astype(f32) * (2.0 * math.pi / (DM * DM))
    cross = jnp.stack([jnp.cos(angle), -jnp.sin(angle)]) * (1.0 / DM)
    local_ids = listed[0, 0, 0] - row_id * (GROUP_ROWS * NYC)
    lane_row = jnp.arange(NYC * GROUP_ROWS, dtype=jnp.int32)
    chosen = (
        (lane_row // GROUP_ROWS)[None, None, :] == jnp.arange(NYC, dtype=jnp.int32)[:, None, None]
    ) & ((lane_row % GROUP_ROWS)[None, None, :] == (local_ids // NYC)[None, :, None])
    chosen = chosen.reshape(NYC * list_len, NYC * GROUP_ROWS).astype(bf16)
    block_of = jnp.tile(local_ids % NYC, NYC)[:, None]
    source = jnp.arange(NYC * BLOCK, dtype=jnp.int32)
    target = NYC * (source % (BLOCK // NYC)) + source // BLOCK
    spread = (target[:, None] == jnp.arange(BLOCK, dtype=jnp.int32)[None, :]).astype(bf16)
    row_high, row_low, turns = row_tables()
    picked = pl.pallas_call(
        spectrum_kernel,
        out_shape=jax.ShapeDtypeStruct((list_len, 2 * BLOCK), bf16),
        scratch_shapes=[pltpu.VMEM((NYC, GROUP_ROWS, 2 * BLOCK), f32)],
        name="spectrum",
    )(partial_rows, cross, turns, row_high, row_low, chosen, block_of, spread)

    entries = lax.all_to_all(
        jnp.broadcast_to(picked[None], (NE,) + picked.shape), "e", 0, 0, tiled=True
    ).reshape(NE * list_len, 2 * BLOCK)
    owner_ids = owners[0, 0, :, :, 0].reshape(-1)
    order = jnp.arange(NE * list_len, dtype=jnp.int32)
    same = (owner_ids[:, None] == owner_ids[None, :]) & (order[:, None] < order[None, :])
    position = owner_ids * capacity + jnp.sum(same.astype(jnp.int32), axis=0)
    place = jnp.arange(ROWS * capacity, dtype=jnp.int32)[:, None] == position[None, :]
    outgoing = dot(place.astype(bf16), entries).astype(bf16)
    outgoing = outgoing.reshape(ROWS, capacity, 2 * BLOCK)
    arrived = lax.all_to_all(outgoing, ROW_AXES, 0, 0, tiled=True)
    return arrived.astype(f32)[None, None]


def solution(mesh):
    split = Mesh(mesh.devices.reshape(NZ, NY, NC, NE), ("z", "y", "c", "e"))
    in_specs = (
        P(None, "e", ROW_AXES, None),
        P(ROW_AXES, "e"),
        P(ROW_AXES + ("e",), None),
        P(),
        P(),
        P(None, ROW_AXES, "e", None),
        P(None, ROW_AXES, None, None, None),
    )
    out_specs = P(None, ROW_AXES, None, None, None)
    return jax.shard_map(shards, mesh=split, in_specs=in_specs, out_specs=out_specs, check_vma=False)
```

time: 362 us -> 174 us (0.48)
  waiting for transfers between devices: 215 us -> 72.8 us
  local copies, waits for them, and re-layouts: 44.1 us -> 9.41 us
  matrix products: 14.3 us -> 0.17 us
  between operations: 13.8 us -> 0.15 us
  starting transfers between devices: 23.1 us -> 35.4 us
  Pallas kernels: 0 us -> 11.8 us
  blocking collectives: 44.2 us -> 34.9 us
    all_gather x2 -> x0, waiting for transfers between devices: 184 us -> none  [the longest x1 105 us: shards(): left_full = lax.all_gather(left_inv, ('row', 'ex'), axis=0, tiled=True)]
    all_to_all x3 -> x5, waiting for transfers between devices: 30.1 us -> 72.8 us  [the longest x1 27.5 us: shards(): factors = lax.all_to_all(factors, ROW_AXES, 0, 0, tiled=True)]
    unnamed x13 -> x11, local copies, waits for them, and re-layouts: 27.9 us -> 1.5 us
    all_gather x2 -> x0, blocking collectives: 20.2 us -> none  [the longest x1 10.7 us: shards(): rows_all = lax.all_gather(own_rows, 'ex', axis=0, tiled=True)]
    dot_general x16 -> x1, matrix products: 14.3 us -> 0.17 us  [dot(): return jnp.dot(a, b, preferred_element_type=f32)]
    all_to_all x3 -> x5, starting transfers between devices: 23.1 us -> 35.4 us  [the longest x1 14.8 us: shards(): factors = lax.all_to_all(factors, ROW_AXES, 0, 0, tiled=True)]
    pallas_call x0 -> x2, Pallas kernels: none -> 11.8 us  [the longest x1 8.55 us: shards(): pl.pallas_call(whiten_kernel, out_shape=jax.ShapeDtypeStruct((ROWS, 2 * G...]
    all_to_all x1 -> x3, blocking collectives: 24 us -> 34.9 us  [the longest x1 20.1 us: shards(): arrived = lax.all_to_all(outgoing, ROW_AXES, 0, 0, tiled=True)]
  transfers between devices with their start and end apart: 5 -> 5, of which waited for: 5 -> 5; matrix products, arithmetic and copies ran while one was open for 2% -> 6% of each run, Pallas kernels for 0% -> 0%
where the time goes in v1:
time: 174 us
  waiting for transfers between devices  72.8 us (42%)
  starting transfers between devices  35.4 us (20%)
  blocking collectives  34.9 us (20%)
  Pallas kernels  11.8 us (7%)
  local copies, waits for them, and re-layouts  9.41 us (5%)
  other arithmetic  8.8 us (5%)
    all_to_all x1, waiting for transfers between devices, shards(): factors = lax.all_to_all(factors, ROW_AXES, 0, 0, tiled=True)  27.5 us
    all_to_all x1, waiting for transfers between devices, shards(): partial_rows = lax.all_to_all(partial_cols, ROW_AXES, 0, 0, tiled=True)  25.3 us
    all_to_all x1, blocking collectives, shards(): arrived = lax.all_to_all(outgoing, ROW_AXES, 0, 0, tiled=True)  20.1 us
    all_to_all x1, starting transfers between devices, shards(): factors = lax.all_to_all(factors, ROW_AXES, 0, 0, tiled=True)  14.8 us
    all_to_all x1, waiting for transfers between devices, shards(): rows = lax.all_to_all(rows, 'y', 0, 0, tiled=True)  13.9 us
    all_to_all x1, blocking collectives, shards(): shared = lax.all_to_all(shared, 'e', 0, 0, tiled=True)  9.46 us
    pallas_call x1, Pallas kernels, shards(): pl.pallas_call(whiten_kernel, out_shape=jax.ShapeDtypeStruct((ROWS, 2 * G...  8.55 us
    all_to_all x1, starting transfers between devices, shards(): rows = lax.all_to_all(rows, 'y', 0, 0, tiled=True)  6.82 us
  transfers between devices with their start and end apart: 5, of which 5 were waited for; matrix products, arithmetic and copies ran while one was open for 6% of the time, Pallas kernels for 0%

profile of v1, /device:TPU:1, one launch (start us, length us, event | category | flops | bytes accessed | tf_op | source)
XLA Modules:
  0.0 173.5 jit_solution(5718201198643241352)
XLA Ops:
  0.0 0.7 reshape.276
  0.7 0.7 pad_maximum_fusion.1
  1.5 9.5 %all_to_all.40 = bf16[4,128,128]{2,1,0:T(8,128)(2,1)S(1)} all-to-all(bf16[4,128,128]{2,1,0:T(8,128)(2,1)S(1)} %broadcast_in_dim.28), channel_id=1, replica_groups=mesh['z'=8,'y'=8,'c'=2,'e'=4] {'e'}, dimensions={0} | all-to-all | bytes 262144 | tf_op jit(solution)/shard_map/all_to_all | solution.py:182
  10.9 1.7 broadcast_in_dim.26
  12.6 6.8 %all-to-all-start = ((bf16[8,16,2048]{2,1,0:T(8,128)(2,1)}), bf16[8,16,2048]{2,1,0:T(8,128)(2,1)S(1)}, u32[]{:S(2)}, u32[]{:S(2)}) async-start(bf16[8,16,2048]{2,1,0:T(8,128)(2,1)} %broadcast_in_dim.26), calls=%async_computation | async-start | bytes 1048576 | tf_op jit(solution)/shard_map/all_to_all | solution.py:194
  19.5 0.1 broadcast_in_dim.32
  19.6 0.1 broadcast_in_dim.30
  19.7 1.1 pad_maximum_fusion
  20.8 13.9 %all-to-all-done = bf16[8,16,2048]{2,1,0:T(8,128)(2,1)S(1)} async-done(((bf16[8,16,2048]{2,1,0:T(8,128)(2,1)}), bf16[8,16,2048]{2,1,0:T(8,128)(2,1)S(1)}, u32[]{:S(2)}, u32[]{:S(2)}) %all-to-all-start) | async-done | bytes 524320 | tf_op jit(solution)/shard_map/all_to_all | solution.py:194
  34.7 14.8 %all-to-all-start.3 = ((bf16[128,32,128]{2,1,0:T(8,128)(2,1)}), bf16[128,32,128]{2,1,0:T(8,128)(2,1)S(1)}, u32[]{:S(2)}, u32[]{:S(2)}) async-start(bf16[128,32,128]{2,1,0:T(8,128)(2,1)} %bitcast.10), calls=%async_computation.3 | async-start | bytes 2097152 | tf_op jit(solution)/shard_map/all_to_all | solution.py:191
  49.6 0.0 copy-start.4
  49.6 0.8 convert_bitcast_fusion
  50.4 1.4 copy.25.row_flip
  51.7 1.3 convert_bitcast_fusion.1.col_flip
  53.0 0.0 copy-done.4
  53.0 27.5 %all-to-all-done.3.rl = bf16[128,32,128]{2,1,0:T(8,128)(2,1)S(1)} async-done(((bf16[128,32,128]{2,1,0:T(8,128)(2,1)}), bf16[128,32,128]{2,1,0:T(8,128)(2,1)S(1)}, u32[]{:S(2)}, u32[]{:S(2)}) %all-to-all-start.3) | async-done | bytes 1048608 | tf_op jit(solution)/shard_map/all_to_all | solution.py:191
  80.5 0.0 copy-start
  80.5 1.3 broadcast_in_dim.27
  81.8 3.7 %all-to-all-start.1 = ((bf16[2,8,16,2048]{3,2,1,0:T(8,128)(2,1)}), bf16[2,8,16,2048]{3,2,1,0:T(8,128)(2,1)S(1)}, u32[]{:S(2)}, u32[]{:S(2)}) async-start(bf16[2,8,16,2048]{3,2,1,0:T(8,128)(2,1)} %broadcast_in_dim.27), calls=%async_computation.1 | async-start | bytes 2097152 | tf_op jit(solution)/shard_map/all_to_all | solution.py:195
  85.5 0.0 copy-done
  85.5 1.7 all-to-all-done.1.gg
  87.2 0.0 copy-start.2
  87.2 0.1 broadcast_in_dim.33
  87.4 5.4 %all_to_all.41.lx = bf16[2,128,16,128]{3,2,1,0:T(8,128)(2,1)} all-to-all(bf16[2,128,16,128]{3,2,1,0:T(8,128)(2,1)S(1)} %broadcast_in_dim.33), channel_id=1, replica_groups=mesh['z'=8,'y'=8,'c'=2,'e'=4] {'c'}, dimensions={0} | all-to-all | bytes 2097152 | tf_op jit(solution)/shard_map/all_to_all | solution.py:199
  92.8 0.0 copy-done.2
  92.8 8.5 %whiten.1 = bf16[128,32,128]{2,1,0:T(8,128)(2,1)} custom-call(bf16[2,8,16,2048]{3,2,1,0:T(8,128)(2,1)} %copy-done.2, bf16[128,32,128]{2,1,0:T(8,128)(2,1)} %copy-done, bf16[2,128,16,128]{3,2,1,0:T(8,128)(2,1)} %all_to_all.41.lx, f32[2048,1]{1,0:T(8,128)} %copy.25.row_flip, f32[1,128]{1,0:T(1,128)} %convert_bitcast_fusion.1.col_flip, ...), custom_call_target="tpu_custom_call" | custom-call | tf_op jit(solution)/shard_map/whiten/pallas_call | solution.py:208
  101.3 0.0 copy-start.3
  101.3 6.8 %all-to-all-start.5 = ((bf16[128,32,128]{2,1,0:T(8,128)(2,1)}), bf16[128,32,128]{2,1,0:T(8,128)(2,1)S(1)}, u32[]{:S(2)}, u32[]{:S(2)}) async-start(bf16[128,32,128]{2,1,0:T(8,128)(2,1)} %whiten.1), calls=%async_computation.5 | async-start | bytes 2097152 | tf_op jit(solution)/shard_map/all_to_all | solution.py:217
  108.1 1.0 broadcast_in_dim_tile.4.block_of
  109.1 0.5 broadcast.331
  109.6 0.0 copy-done.3
  109.6 0.7 reduce.3
  110.3 0.1 reshape_squeeze.3
  110.4 0.1 convert_reduce_fusion
  110.5 0.5 fusion.1
  111.1 0.7 maximum_multiply_fusion.cross
  111.8 0.1 broadcast_compare_fusion
  111.9 0.8 and_convert_fusion
  112.7 1.1 fusion.spread
  113.8 25.3 %all-to-all-done.5.parts = bf16[128,32,128]{2,1,0:T(8,128)(2,1)S(1)} async-done(((bf16[128,32,128]{2,1,0:T(8,128)(2,1)}), bf16[128,32,128]{2,1,0:T(8,128)(2,1)S(1)}, u32[]{:S(2)}, u32[]{:S(2)}) %all-to-all-start.5) | async-done | bytes 1048608 | tf_op jit(solution)/shard_map/all_to_all | solution.py:217
  139.1 0.0 copy-start.1
  139.1 1.0 copy-done.1
  140.0 3.3 %spectrum.1 = bf16[32,256]{1,0:T(8,128)(2,1)} custom-call(bf16[128,32,128]{2,1,0:T(8,128)(2,1)} %copy-done.1, f32[2,16,16,128]{3,2,1,0:T(8,128)} %maximum_multiply_fusion.cross, f32[2,16,1,128]{3,2,1,0:T(1,128)} %constant.137.clone.turns, bf16[256,256]{1,0:T(8,128)(2,1)} %constant.138.clone.high, bf16[256,256]{1,0:T(8,128)(2,1)} %constant.139.clone.low, ...), custom_call_target="tpu_custom_call" | custom-call | tf_op jit(solution)/shard_map/spectrum/pallas_call | solution.py:235
  143.3 1.4 broadcast_in_dim.34
  144.7 3.3 %all-to-all-start.6 = ((bf16[4,32,256]{2,1,0:T(8,128)(2,1)}), bf16[4,32,256]{2,1,0:T(8,128)(2,1)S(1)}, u32[]{:S(2)}, u32[]{:S(2)}) async-start(bf16[4,32,256]{2,1,0:T(8,128)(2,1)} %broadcast_in_dim.34), calls=%async_computation.6 | async-start | bytes 131072 | tf_op jit(solution)/shard_map/all_to_all | solution.py:242
  148.0 4.4 %all-to-all-done.6 = bf16[4,32,256]{2,1,0:T(8,128)(2,1)S(1)} async-done(((bf16[4,32,256]{2,1,0:T(8,128)(2,1)}), bf16[4,32,256]{2,1,0:T(8,128)(2,1)S(1)}, u32[]{:S(2)}, u32[]{:S(2)}) %all-to-all-start.6) | async-done | bytes 65568 | tf_op jit(solution)/shard_map/all_to_all | solution.py:242
  152.4 0.2 convolution_convert_fusion
  152.6 0.1 reshape.286
  152.6 20.1 %all_to_all.42 = bf16[128,2,256]{2,1,0:T(2,128)(2,1)S(1)} all-to-all(bf16[128,2,256]{2,1,0:T(2,128)(2,1)S(1)} %reshape.286), channel_id=1, replica_groups=mesh['z'=8,'y'=8,'c'=2,'e'=4] {'z','y','c'}, dimensions={0} | all-to-all | bytes 262144 | tf_op jit(solution)/shard_map/all_to_all | solution.py:252
  172.7 0.8 bitcast_convert_fusion
  (15 shorter events, 0.2 us)
Async XLA Ops:
  12.6 22.1 %all-to-all-start = ((bf16[8,16,2048]{2,1,0:T(8,128)(2,1)}), bf16[8,16,2048]{2,1,0:T(8,128)(2,1)S(1)}, u32[]{:S(2)}, u32[]{:S(2)}) async-start(bf16[8,16,2048]{2,1,0:T(8,128)(2,1)} %broadcast_in_dim.26), calls=%async_computation | async-start | bytes 1048576 | tf_op jit(solution)/shard_map/all_to_all | solution.py:194
  34.7 45.8 %all-to-all-start.3 = ((bf16[128,32,128]{2,1,0:T(8,128)(2,1)}), bf16[128,32,128]{2,1,0:T(8,128)(2,1)S(1)}, u32[]{:S(2)}, u32[]{:S(2)}) async-start(bf16[128,32,128]{2,1,0:T(8,128)(2,1)} %bitcast.10), calls=%async_computation.3 | async-start | bytes 2097152 | tf_op jit(solution)/shard_map/all_to_all | solution.py:191
  49.6 3.4 %copy-start.4 = (s32[1,1,1,32]{3,2,1,0:T(1,128)S(1)}, s32[1,1,1,32]{3,2,1,0:T(1,128)}, u32[]{:S(2)}) copy-start(s32[1,1,1,32]{3,2,1,0:T(1,128)} %param.18) | copy-start | bytes 388
  80.5 5.0 %copy-start = (bf16[128,32,128]{2,1,0:T(8,128)(2,1)}, bf16[128,32,128]{2,1,0:T(8,128)(2,1)S(1)}, u32[]{:S(2)}) copy-start(bf16[128,32,128]{2,1,0:T(8,128)(2,1)S(1)} %all-to-all-done.3.rl) | copy-start | bytes 3145732
  81.8 5.5 %all-to-all-start.1 = ((bf16[2,8,16,2048]{3,2,1,0:T(8,128)(2,1)}), bf16[2,8,16,2048]{3,2,1,0:T(8,128)(2,1)S(1)}, u32[]{:S(2)}, u32[]{:S(2)}) async-start(bf16[2,8,16,2048]{3,2,1,0:T(8,128)(2,1)} %broadcast_in_dim.27), calls=%async_computation.1 | async-start | bytes 2097152 | tf_op jit(solution)/shard_map/all_to_all | solution.py:195
  87.2 5.5 %copy-start.2 = (bf16[2,8,16,2048]{3,2,1,0:T(8,128)(2,1)}, bf16[2,8,16,2048]{3,2,1,0:T(8,128)(2,1)S(1)}, u32[]{:S(2)}) copy-start(bf16[2,8,16,2048]{3,2,1,0:T(8,128)(2,1)S(1)} %all-to-all-done.1.gg) | copy-start | bytes 3145732
  101.3 8.3 %copy-start.3 = (s32[1,1,4,32,1]{3,4,2,1,0:T(1,128)S(1)}, s32[1,1,4,32,1]{3,4,2,1,0:T(1,128)}, u32[]{:S(2)}) copy-start(s32[1,1,4,32,1]{3,4,2,1,0:T(1,128)} %param.19) | copy-start | bytes 1540
  101.3 37.8 %all-to-all-start.5 = ((bf16[128,32,128]{2,1,0:T(8,128)(2,1)}), bf16[128,32,128]{2,1,0:T(8,128)(2,1)S(1)}, u32[]{:S(2)}, u32[]{:S(2)}) async-start(bf16[128,32,128]{2,1,0:T(8,128)(2,1)} %whiten.1), calls=%async_computation.5 | async-start | bytes 2097152 | tf_op jit(solution)/shard_map/all_to_all | solution.py:217
  139.1 1.0 copy-start.1
  144.7 7.7 %all-to-all-start.6 = ((bf16[4,32,256]{2,1,0:T(8,128)(2,1)}), bf16[4,32,256]{2,1,0:T(8,128)(2,1)S(1)}, u32[]{:S(2)}, u32[]{:S(2)}) async-start(bf16[4,32,256]{2,1,0:T(8,128)(2,1)} %broadcast_in_dim.34), calls=%async_computation.6 | async-start | bytes 131072 | tf_op jit(solution)/shard_map/all_to_all | solution.py:242
